TPU v7x, 32 devices: a whole 2x2x4 slice. The times are simulated.
32 devices in a mesh: ctx: 8 (over z, core), tp: 4 (over y, x).
Axes of the slice: x: 2, y: 2, z: 4, core: 2. Of those that a mesh axis runs over, the one named last changes fastest.
Arguments:
- hidden_rows: bfloat16 [4096, 8192], P('ctx', 'tp'), may hold values from -6 to 6
- w_value: bfloat16 [8192, 8192], P('ctx', 'tp'), may hold values from -0.0625 to 0.0625
- w_gate: bfloat16 [8192, 8192], P('ctx', 'tp'), may hold values from -0.0625 to 0.0625
- state_proj: bfloat16 [4096, 2, 4, 256], P('ctx'), may hold values from -1.5 to 1.5
- rates: float32 [4096, 128], P('ctx', 'tp'), may hold values from 0 to 4.5, as said below
- read_weights: float32 [6, 4096, 128], P(None, 'ctx', 'tp'), may hold values from 0.25 to 2
- prior_state: float32 [128, 64, 256], P('tp'), may hold values from -24 to 24
- skip_weight: float32 [128], P('tp'), may hold values from 0.5 to 2
- norm_gain: float32 [8192], P('tp'), may hold values from 0.25 to 1.75
Outputs:
- layer_out: bfloat16 [4096, 8192], P('ctx', 'tp')
Inputs may be any that keep to these rules, and one draw needn't show every extreme that they name: Positive rates.
All inputs are finite; a program needn't handle non-finite values.
Results may differ from a plain program's by a relative error of at most 0.0085.
Values may be sent and summed in bfloat16 or wider, within the bound.
A program may use at most 128 MiB of HBM per device.

v0:
```python
import jax
import jax.numpy as jnp
from jax import lax
from jax.sharding import PartitionSpec as P

HEAD_DIM = 64
STATE = 256
HPG = 32
LEVELS = 6


def swapped(value, axis, distance):
    return lax.ppermute(value, axis, [(i, i ^ 1 << distance) for i in range(lax.axis_size(axis))])


def on_device(
    hidden_rows,
    w_value,
    w_gate,
    state_proj,
    rates,
    read_weights,
    prior_state,
    skip_weight,
    norm_gain,
):
    tok_rows = rates.shape[0]
    head_count = rates.shape[1]
    level_total = LEVELS - 2
    full_rows = lax.all_gather(hidden_rows, "tp", axis=1, tiled=True)
    value_sum = jnp.dot(
        full_rows,
        lax.all_gather(w_value, "ctx", axis=0, tiled=True),
        preferred_element_type=jnp.float32,
    )
    gate_sum = jnp.dot(
        full_rows,
        lax.all_gather(w_gate, "ctx", axis=0, tiled=True),
        preferred_element_type=jnp.float32,
    )
    values_proj = value_sum.astype(jnp.bfloat16)
    gates_proj = gate_sum.astype(jnp.bfloat16)
    values3 = values_proj.reshape(tok_rows, head_count, HEAD_DIM)
    group_index = lax.axis_index("tp") * head_count // HPG
    write_vec = lax.dynamic_index_in_dim(state_proj[:, 0], group_index, 1, keepdims=False)
    read_vec = lax.dynamic_index_in_dim(state_proj[:, 1], group_index, 1, keepdims=False)
    cum_rate = jnp.cumsum(rates, axis=0)
    scores = lax.dot_general(
        read_vec, write_vec, (((1,), (1,)), ((), ())), preferred_element_type=jnp.float32
    )
    rate_lag = cum_rate.T[:, :, None] - cum_rate.T[:, None, :]
    causal = (jnp.arange(tok_rows)[:, None] >= jnp.arange(tok_rows)[None, :])[None]
    mixing = (
        jnp.where(causal, jnp.exp(-jnp.where(causal, rate_lag, 0.0)), 0.0) * scores[None]
    ).astype(jnp.bfloat16)
    local_out = jnp.einsum("hts,shp->thp", mixing, values3, preferred_element_type=jnp.float32)
    span_total = cum_rate[-1]
    write_weighted = (
        jnp.exp(-(span_total[None] - cum_rate))[:, :, None]
        * write_vec[:, None, :].astype(jnp.float32)
    ).astype(jnp.bfloat16)
    end_state = jnp.einsum(
        "thn,thp->hpn", write_weighted, values3, preferred_element_type=jnp.float32
    )
    my_block = lax.axis_index("ctx")
    agg_state = end_state
    agg_rate = span_total
    start_rate = jnp.zeros((head_count,), jnp.float32)
    tier_components = []
    for bit_pos in range(lax.axis_size("ctx").bit_length() - 1):
        other_state, other_rate = swapped((agg_state, agg_rate), "ctx", bit_pos)
        is_upper = jnp.right_shift(my_block, bit_pos) % 2 == 1
        tier_components.append(
            jnp.where(is_upper, other_state * jnp.exp(-start_rate)[:, None, None], 0.0)
        )
        agg_state = jnp.where(
            is_upper,
            other_state * jnp.exp(-agg_rate)[:, None, None] + agg_state,
            agg_state * jnp.exp(-other_rate)[:, None, None] + other_state,
        )
        agg_rate = agg_rate + other_rate
        start_rate = jnp.where(is_upper, start_rate + other_rate, start_rate)
    for extra_level in range(level_total - len(tier_components)):
        tier_components.append(jnp.zeros((head_count, HEAD_DIM, STATE), jnp.float32))
    carried = jnp.stack(tier_components)
    prior_part = jnp.exp(-start_rate)[:, None, None] * prior_state
    states = jnp.concatenate([carried, prior_part[None]], axis=0)
    projected = jnp.einsum(
        "tn,lhpn->tlhp", read_vec.astype(jnp.float32), states, precision=lax.Precision.HIGHEST
    )
    read_scale = read_weights[1:] * jnp.exp(-cum_rate)[None]
    carried_out = jnp.einsum(
        "lth,tlhp->thp", read_scale, projected, precision=lax.Precision.HIGHEST
    )
    mixed_out = (
        read_weights[0][:, :, None] * local_out
        + carried_out
        + skip_weight[None, :, None] * values3.astype(jnp.float32)
    )
    gates3 = gates_proj.reshape(tok_rows, head_count, HEAD_DIM).astype(jnp.float32)
    filtered_result = mixed_out * jax.nn.silu(gates3)
    inverse = lax.rsqrt(jnp.mean(filtered_result * filtered_result, axis=2, keepdims=True) + 1e-05)
    result = filtered_result * inverse * norm_gain.reshape(head_count, HEAD_DIM)[None]
    return result.reshape(tok_rows, head_count * HEAD_DIM).astype(jnp.bfloat16)


def solution(mesh):
    in_specs = (
        P("ctx", "tp"),
        P("ctx", "tp"),
        P("ctx", "tp"),
        P("ctx", None, None, None),
        P("ctx", "tp"),
        P(None, "ctx", "tp"),
        P("tp", None, None),
        P("tp"),
        P("tp"),
    )
    out_specs = P("ctx", "tp")
    return jax.shard_map(
        on_device, mesh=mesh, in_specs=in_specs, out_specs=out_specs, check_vma=False
    )
```

profile of v0, /device:TPU:17, one launch (start us, length us, event | category | flops | bytes accessed | tf_op | source)
XLA Modules:
  0.0 836.5 jit_solution(6695829626215990275)
XLA Ops:
  6.5 0.0 all-gather.4.cloned.1.call-start
  6.5 0.7 all-gather.4.cloned.1.call-update
  7.3 0.0 all-gather.6.cloned.1.call-start
  7.3 0.7 all-gather.6.cloned.1.call-update
  8.0 0.0 all-gather.8.cloned.1.call-start
  8.1 0.7 all-gather.8.cloned.1.call-update
  8.8 1.2 reduce-window.6
  10.0 0.2 slice_reduce_fusion
  10.2 0.7 copy_bitcast_fusion.2
  10.9 0.2 slice_reduce_fusion.1
  11.1 0.7 fusion.19
  11.8 1.1 constant_dynamic-slice_fusion
  12.9 0.7 negate_exponential_fusion
  13.6 0.9 fusion.12
  14.5 83.1 %all-gather.4.cloned.1.call-done = bf16[512,8192]{1,0:T(8,128)(2,1)} async-done(((bf16[512,2048]{1,0:T(8,128)(2,1)}), bf16[512,8192]{1,0:T(8,128)(2,1)}) %all-gather.4.cloned.1.call-update) | async-done | bytes 8388624 | tf_op jit(solution)/shard_map/all_gather | solution.py:30
  97.6 289.0 %all-gather.6.cloned.1.call-done = bf16[8192,2048]{1,0:T(8,128)(2,1)} async-done(((bf16[1024,2048]{1,0:T(8,128)(2,1)}), bf16[8192,2048]{1,0:T(8,128)(2,1)}) %all-gather.6.cloned.1.call-update) | async-done | bytes 33554448 | tf_op jit(solution)/shard_map/all_gather | solution.py:33
  386.6 25.6 %convolution_convert_fusion.1 = bf16[512,2048]{1,0:T(8,128)(2,1)} fusion(bf16[512,8192]{1,0:T(8,128)(2,1)} %all-gather.4.cloned.1.call-done, bf16[8192,2048]{1,0:T(8,128)(2,1)} %all-gather.6.cloned.1.call-done), kind=kOutput, calls=%fused_computation.16 | convolution fusion | flops 17180917760 | bytes 44040192 | tf_op jit(solution)/shard_map/dot_general | solution.py:31
  412.2 2.9 copy.27
  415.1 0.0 copy-start.6
  415.1 1.3 copy-done.6
  416.4 5.1 fusion.2
  421.5 0.3 collective-permute-start
  421.8 0.2 collective-permute-start.1
  422.0 3.9 collective-permute-done.1
  425.9 0.5 negate_exponential_fusion.4
  426.4 0.0 collective-permute-start.3
  426.4 3.0 collective-permute-done.3
  429.4 0.6 add.71
  430.0 1.7 collective-permute-start.5
  431.7 2.3 collective-permute-done.5
  434.0 1.2 fusion.16
  435.3 0.0 collective-permute-done
  435.3 1.3 copy-done.2
  436.6 3.4 add_select_fusion.1
  440.0 2.6 collective-permute-start.2
  442.6 0.8 mul.166
  443.4 0.8 iota_compare_fusion
  444.1 0.6 slice_bitcast_fusion
  444.8 1.6 multiply_bitcast_fusion
  446.4 1.3 fusion.10
  447.7 0.7 negate_exponential_fusion.2
  448.3 188.4 %collective-permute-done.2 = f32[32,64,256]{2,1,0:T(8,128)S(1)} collective-permute-done((f32[32,64,256]{2,1,0:T(8,128)}, f32[32,64,256]{2,1,0:T(8,128)S(1)}, u32[]{:S(2)}, u32[]{:S(2)}) %collective-permute-start.2) | collective-permute-done | bytes 2097184 | tf_op jit(solution)/shard_map/ppermute | solution.py:13
  636.8 3.4 add_select_fusion
  640.1 4.6 collective-permute-start.4
  644.7 120.0 %all-gather.8.cloned.1.call-done = bf16[8192,2048]{1,0:T(8,128)(2,1)} async-done(((bf16[1024,2048]{1,0:T(8,128)(2,1)}), bf16[8192,2048]{1,0:T(8,128)(2,1)}) %all-gather.8.cloned.1.call-update) | async-done | bytes 33554448 | tf_op jit(solution)/shard_map/all_gather | solution.py:38
  764.8 24.8 %fusion.8 = f32[512,2048]{1,0:T(8,128)} fusion(bf16[512,8192]{1,0:T(8,128)(2,1)} %all-gather.4.cloned.1.call-done, bf16[8192,2048]{1,0:T(8,128)(2,1)} %all-gather.8.cloned.1.call-done), kind=kOutput, calls=%fused_computation.15 | convolution fusion | flops 17181966336 | bytes 46137344 | tf_op jit(solution)/shard_map/dot_general | solution.py:36
  789.5 5.3 copy.32
  794.9 1.8 bitcast_dynamic-update-slice_fusion.3
  796.7 0.2 bitcast_dynamic-update-slice_fusion.2
  796.9 0.0 copy-start.5
  796.9 0.0 collective-permute-done.4
  796.9 1.9 bitcast_dynamic-update-slice_fusion.1
  798.9 0.0 copy-start.10
  798.9 0.1 broadcast_dynamic-update-slice_fusion
  799.0 0.1 copy-done.5
  799.1 0.2 bitcast_dynamic-update-slice_fusion
  799.3 0.6 copy-done.10
  799.9 0.0 copy-start.17
  800.0 13.2 %multiply_reduce_fusion = f32[512,32,64]{0,2,1:T(8,128)} fusion(f32[512,32,5]{0,1,2:T(8,128)S(1)} %copy-done.10, f32[5,32,64,256]{3,2,1,0:T(8,128)S(1)} %bitcast_dynamic-update-slice_fusion, bf16[512,1,1,256]{3,2,1,0:T(2,128)(2,1)S(1)} %get-tuple-element.22), kind=kOutput, calls=%fused_computation.1 | convolution fusion | flops 16115564544 | bytes 15269888 | tf_op jit(solution)/shard_map/tn,lhpn->tlhp/dot_general | solution.py:88
  813.1 0.0 copy-done.3
  813.2 13.6 %multiply_reduce_fusion.1 = (f32[512,32]{0,1:T(8,128)S(1)}, f32[512,32,64]{0,2,1:T(8,128)S(1)}) fusion(f32[512,32,64]{0,2,1:T(8,128)S(1)} %bitcast.69, bf16[512,32,64]{0,2,1:T(8,128)(2,1)S(1)} %bitcast.71, f32[32]{0:T(128)S(1)} %copy-done.17, f32[512,32,64]{0,2,1:T(8,128)} %multiply_reduce_fusion, f32[512,512]{1,0:T(8,128)S(1)} %copy-done.8, ...), kind=kOutput, calls=%fused_computation.13 | convolution fusion | flops 1136640000 | bytes 16187520 | tf_op jit(solution)/shard_map/hts,shp->thp/dot_general | solution.py:56
  826.8 0.0 copy-start.1
  826.8 0.7 multiply_convert_fusion.4
  827.5 2.4 copy.33
  (30 shorter events, 0.1 us)
Async XLA Ops:
  6.5 2.2 copy-start
  6.5 91.1 %all-gather.4.cloned.1.call-start = ((), (), s32[]{:S(2)}) async-start(), calls=%async_computation | async-start | bytes 10485760 | tf_op jit(solution)/shard_map/all_gather | solution.py:30
  7.3 3.8 copy-start.4
  7.3 379.3 %all-gather.6.cloned.1.call-start = ((), (), s32[]{:S(2)}) async-start(), calls=%async_computation.1 | async-start | bytes 37748736 | tf_op jit(solution)/shard_map/all_gather | solution.py:33
  8.0 756.7 %all-gather.8.cloned.1.call-start = ((), (), s32[]{:S(2)}) async-start(), calls=%async_computation.2 | async-start | bytes 37748736 | tf_op jit(solution)/shard_map/all_gather | solution.py:38
  415.1 1.3 copy-start.6
  421.5 22.6 %copy-start.9 = (f32[6,512,32]{1,2,0:T(8,128)S(1)}, f32[6,512,32]{1,2,0:T(8,128)}, u32[]{:S(2)}) copy-start(f32[6,512,32]{1,2,0:T(8,128)} %param.14) | copy-start | bytes 1179652
  421.5 13.8 %collective-permute-start = (f32[32,64,256]{2,1,0:T(8,128)}, f32[32,64,256]{2,1,0:T(8,128)S(1)}, u32[]{:S(2)}, u32[]{:S(2)}) collective-permute-start(f32[32,64,256]{2,1,0:T(8,128)} %fusion.2), channel_id=1, source_target_pairs={{0,4},{4,0},{8,12},{12,8},{16,20},{20,16},{24,28},{28,24},{1,5},{5... | collective-permute-start | bytes 6291464 | tf_op jit(solution)/shard_map/ppermute | solution.py:13
  421.8 4.1 collective-permute-start.1
  426.4 3.0 collective-permute-start.3
  429.4 2.3 copy-start.16
  430.0 4.1 collective-permute-start.5
  435.3 1.3 copy-start.2
  440.0 196.8 %collective-permute-start.2 = (f32[32,64,256]{2,1,0:T(8,128)}, f32[32,64,256]{2,1,0:T(8,128)S(1)}, u32[]{:S(2)}, u32[]{:S(2)}) collective-permute-start(f32[32,64,256]{2,1,0:T(8,128)} %add_select_fusion.1), channel_id=1, source_target_pairs={{0,8},{4,12},{8,0},{12,4},{16,24},{20,28},{24,16},{28,20},{1,9},{5... | collective-permute-start | bytes 6291464 | tf_op jit(solution)/shard_map/ppermute | solution.py:13
  640.1 156.8 %collective-permute-start.4 = (f32[32,64,256]{2,1,0:T(8,128)}, f32[32,64,256]{2,1,0:T(8,128)}, u32[]{:S(2)}, u32[]{:S(2)}) collective-permute-start(f32[32,64,256]{2,1,0:T(8,128)} %add_select_fusion), channel_id=1, source_target_pairs={{0,16},{4,20},{8,24},{12,28},{16,0},{20,4},{24,8},{28,12},{1,17},{... | collective-permute-start | bytes 6291464 | tf_op jit(solution)/shard_map/ppermute | solution.py:13
  794.9 1.8 copy-start.15
  796.9 2.2 copy-start.5
  796.9 2.2 copy-start.14
  798.9 1.0 copy-start.10
  799.9 13.2 %copy-start.3 = (f32[512,2048]{0,1:T(8,128)S(1)}, f32[512,2048]{0,1:T(8,128)}, u32[]{:S(2)}) copy-start(f32[512,2048]{0,1:T(8,128)} %copy.32) | copy-start | bytes 12582916
  799.9 13.2 %copy-start.7 = (bf16[512,2048]{0,1:T(8,128)(2,1)S(1)}, bf16[512,2048]{0,1:T(8,128)(2,1)}, u32[]{:S(2)}) copy-start(bf16[512,2048]{0,1:T(8,128)(2,1)} %copy-done.6) | copy-start | bytes 6291460
  799.9 13.2 %copy-start.8 = (f32[512,512]{1,0:T(8,128)S(1)}, f32[512,512]{1,0:T(8,128)}, u32[]{:S(2)}) copy-start(f32[512,512]{1,0:T(8,128)} %fusion.10) | copy-start | bytes 3145732
  799.9 13.2 %copy-start.11 = (pred[512,512]{1,0:T(8,128)(4,1)S(1)}, pred[512,512]{1,0:T(8,128)(4,1)}, u32[]{:S(2)}) copy-start(pred[512,512]{1,0:T(8,128)(4,1)} %iota_compare_fusion) | copy-start | bytes 786436
  799.9 13.2 %copy-start.12 = (f32[32,512]{1,0:T(8,128)S(1)}, f32[32,512]{1,0:T(8,128)}, u32[]{:S(2)}) copy-start(f32[32,512]{1,0:T(8,128)} %get-tuple-element.11) | copy-start | bytes 196612
  799.9 13.2 %copy-start.13 = (f32[512,32]{0,1:T(8,128)S(1)}, f32[512,32]{0,1:T(8,128)}, u32[]{:S(2)}) copy-start(f32[512,32]{0,1:T(8,128)} %slice_bitcast_fusion) | copy-start | bytes 196612
  799.9 13.2 %copy-start.17 = (f32[32]{0:T(128)S(1)}, f32[32]{0:T(128)}, u32[]{:S(2)}) copy-start(f32[32]{0:T(128)} %param.16) | copy-start | bytes 388
  826.8 3.1 copy-start.1
Sparse Core Ops, SparseCore 0:
  9.2 88.3 all-gather.3
  99.2 287.3 all-gather.5
  388.2 376.4 all-gather.7
where the time goes:
time: 837 us; the launch traced here: 836 us
  waiting for transfers between devices  692 us (83%)
  matrix products  83.6 us (10%)
  other arithmetic  20.6 us (2%)
  local copies, waits for them, and re-layouts  17.6 us (2%)
  between operations  13.4 us (2%)
  starting transfers between devices  9.53 us (1%)
    all_gather x1, waiting for transfers between devices, on_device(): lax.all_gather(w_value, 'ctx', axis=0, tiled=True)  289 us
    ppermute x6, waiting for transfers between devices, swapped(): lax.ppermute(value, axis, [(i, i ^ 1 << distance) for i in range(lax.axis...  198 us
    all_gather x1, waiting for transfers between devices, on_device(): lax.all_gather(w_gate, 'ctx', axis=0, tiled=True)  120 us
    all_gather x1, waiting for transfers between devices, on_device(): full_rows = lax.all_gather(hidden_rows, 'tp', axis=1, tiled=True)  83.1 us
    dot_general x1, matrix products, on_device(): jnp.dot(full_rows, lax.all_gather(w_value, 'ctx', axis=0, tiled=True), pr...  25.6 us
    dot_general x1, matrix products, on_device(): jnp.dot(full_rows, lax.all_gather(w_gate, 'ctx', axis=0, tiled=True), pre...  24.8 us
  transfers between devices with their start and end apart: 9, of which 7 were waited for; matrix products, arithmetic and copies ran while one was open for 10% of the time, Pallas kernels for 0%

commit v1 on v0

--- a/solution.py
+++ b/solution.py
@@ -7,6 +7,18 @@
 STATE = 256
 HPG = 32
 LEVELS = 6
+
+
+def ring_gather(shard, axis, dim):
+    ways, here, step = (lax.axis_size(axis), lax.axis_index(axis), shard.shape[dim])
+    lengths = [n * ways if d == dim else n for d, n in enumerate(shard.shape)]
+    full = lax.dynamic_update_slice_in_dim(
+        jnp.zeros(lengths, shard.dtype), shard, here * step, axis=dim
+    )
+    for far in range(1, ways):
+        shard = lax.ppermute(shard, axis, [(d, (d + 1) % ways) for d in range(ways)])
+        full = lax.dynamic_update_slice_in_dim(full, shard, (here - far) % ways * step, axis=dim)
+    return full
 
 
 def swapped(value, axis, distance):
@@ -27,7 +39,7 @@
     tok_rows = rates.shape[0]
     head_count = rates.shape[1]
     level_total = LEVELS - 2
-    full_rows = lax.all_gather(hidden_rows, "tp", axis=1, tiled=True)
+    full_rows = ring_gather(hidden_rows, "tp", 1)
     value_sum = jnp.dot(
         full_rows,
         lax.all_gather(w_value, "ctx", axis=0, tiled=True),

time: 837 us -> 790 us (0.944)
  waiting for transfers between devices: 692 us -> 628 us
  local copies, waits for them, and re-layouts: 17.6 us -> 35.6 us
    all_gather x1, waiting for transfers between devices: 120 us -> 278 us  [on_device(): lax.all_gather(w_gate, 'ctx', axis=0, tiled=True)]
    all_gather x1, waiting for transfers between devices: 289 us -> 145 us  [on_device(): lax.all_gather(w_value, 'ctx', axis=0, tiled=True)]
    ppermute x0 -> x3, waiting for transfers between devices: none -> 121 us  [ring_gather(): lax.ppermute(shard, axis, [(d, (d + 1) % ways) for d in range(ways)])]
    ppermute x6, waiting for transfers between devices: 198 us -> 81.2 us  [swapped(): lax.ppermute(value, axis, [(i, i ^ 1 << distance) for i in range(lax.axis...]
    all_gather x1 -> x0, waiting for transfers between devices: 83.1 us -> none  [on_device(): full_rows = lax.all_gather(hidden_rows, 'tp', axis=1, tiled=True)]
    dynamic_update_slice x0 -> x4, local copies, waits for them, and re-layouts: none -> 11.2 us  [the longest x3 9.73 us: ring_gather(): lax.dynamic_update_slice_in_dim(full, shard, (here - far) % ways * step,...]
  transfers between devices with their start and end apart: 9 -> 11, of which waited for: 7 -> 8; matrix products, arithmetic and copies ran while one was open for 10% -> 14% of each run, Pallas kernels for 0% -> 0%
where the time goes in v1:
time: 790 us; the launch traced here: 785 us
  waiting for transfers between devices  628 us (79%)
  matrix products  81 us (10%)
  local copies, waits for them, and re-layouts  35.6 us (5%)
  other arithmetic  19.5 us (2%)
  between operations  13.7 us (2%)
    all_gather x1, waiting for transfers between devices, on_device(): lax.all_gather(w_gate, 'ctx', axis=0, tiled=True)  278 us
    all_gather x1, waiting for transfers between devices, on_device(): lax.all_gather(w_value, 'ctx', axis=0, tiled=True)  145 us
    ppermute x3, waiting for transfers between devices, ring_gather(): lax.ppermute(shard, axis, [(d, (d + 1) % ways) for d in range(ways)])  121 us
    ppermute x6, waiting for transfers between devices, swapped(): lax.ppermute(value, axis, [(i, i ^ 1 << distance) for i in range(lax.axis...  81.2 us
    dot_general x1, matrix products, on_device(): jnp.dot(full_rows, lax.all_gather(w_value, 'ctx', axis=0, tiled=True), pr...  25.6 us
    dot_general x1, matrix products, on_device(): jnp.dot(full_rows, lax.all_gather(w_gate, 'ctx', axis=0, tiled=True), pre...  24.8 us
  transfers between devices with their start and end apart: 11, of which 8 were waited for; matrix products, arithmetic and copies ran while one was open for 14% of the time, Pallas kernels for 0%

profile of v1, /device:TPU:17, one launch (start us, length us, event | category | flops | bytes accessed | tf_op | source)
XLA Modules:
  0.0 785.4 jit_solution(15474561695922368310)
XLA Ops:
  6.5 0.7 all-gather.3.cloned.1.call-update
  7.3 0.0 all-gather.5.cloned.1.call-start
  7.3 0.7 all-gather.5.cloned.1.call-update
  8.0 1.3 collective-permute-start
  9.3 46.5 %collective-permute-done = bf16[512,2048]{1,0:T(8,128)(2,1)} collective-permute-done((bf16[512,2048]{1,0:T(8,128)(2,1)}, bf16[512,2048]{1,0:T(8,128)(2,1)}, u32[]{:S(2)}, u32[]{:S(2)}) %collective-permute-start) | collective-permute-done | bytes 2097184 | tf_op jit(solution)/shard_map/ppermute | solution.py:19
  55.8 0.3 collective-permute-start.1
  56.1 1.2 reduce-window.6
  57.3 45.4 %collective-permute-done.1 = bf16[512,2048]{1,0:T(8,128)(2,1)} collective-permute-done((bf16[512,2048]{1,0:T(8,128)(2,1)}, bf16[512,2048]{1,0:T(8,128)(2,1)}, u32[]{:S(2)}, u32[]{:S(2)}) %collective-permute-start.1) | collective-permute-done | bytes 2097184 | tf_op jit(solution)/shard_map/ppermute | solution.py:19
  102.7 0.0 collective-permute-start.2
  102.7 0.2 slice_reduce_fusion
  103.0 0.7 copy_bitcast_fusion.2
  103.7 0.2 slice_reduce_fusion.1
  103.9 1.7 fusion.20
  105.6 0.5 constant_dynamic-slice_fusion
  106.1 0.7 negate_exponential_fusion
  106.9 0.0 copy-start.8
  106.9 4.2 broadcast_in_dim.30
  111.1 1.5 constant_dynamic-update-slice_fusion.3
  112.6 3.2 constant_dynamic-update-slice_fusion.2
  115.8 3.3 constant_dynamic-update-slice_fusion.1
  119.1 29.6 %collective-permute-done.2 = bf16[512,2048]{1,0:T(8,128)(2,1)} collective-permute-done((bf16[512,2048]{1,0:T(8,128)(2,1)}, bf16[512,2048]{1,0:T(8,128)(2,1)}, u32[]{:S(2)}, u32[]{:S(2)}) %collective-permute-start.2) | collective-permute-done | bytes 2097184 | tf_op jit(solution)/shard_map/ppermute | solution.py:19
  148.7 3.2 constant_dynamic-update-slice_fusion
  151.9 145.3 %all-gather.3.cloned.1.call-done = bf16[8192,2048]{1,0:T(8,128)(2,1)} async-done(((bf16[1024,2048]{1,0:T(8,128)(2,1)}), bf16[8192,2048]{1,0:T(8,128)(2,1)}) %all-gather.3.cloned.1.call-update) | async-done | bytes 33554448 | tf_op jit(solution)/shard_map/all_gather | solution.py:45
  297.3 25.6 %convolution_convert_fusion.1 = bf16[512,2048]{1,0:T(8,128)(2,1)} fusion(bf16[512,8192]{1,0:T(8,128)(2,1)} %constant_dynamic-update-slice_fusion, bf16[8192,2048]{1,0:T(8,128)(2,1)} %all-gather.3.cloned.1.call-done), kind=kOutput, calls=%fused_computation.16 | convolution fusion | flops 17180917760 | bytes 44040192 | tf_op jit(solution)/shard_map/dot_general | solution.py:43
  322.9 2.9 copy.27
  325.8 1.3 copy-done.5
  327.1 4.0 fusion.2
  331.1 0.3 collective-permute-start.3
  331.3 0.2 collective-permute-start.4
  331.6 0.8 iota_compare_fusion
  332.4 1.8 constant_dynamic-slice_fusion.1
  334.1 0.8 slice_bitcast_fusion
  335.0 1.0 multiply_bitcast_fusion
  336.0 1.3 fusion.10
  337.3 0.0 collective-permute-done.4
  337.3 0.1 collective-permute-start.6
  337.4 2.9 collective-permute-done.6
  340.3 1.7 collective-permute-start.8
  342.1 0.0 copy-done.13
  342.1 0.1 mul.182
  342.1 2.1 collective-permute-done.8
  344.2 0.0 collective-permute-done.3
  344.2 0.0 copy-start.3
  344.2 1.3 copy-done.3
  345.6 3.4 add_select_fusion.1
  349.0 3.0 collective-permute-start.5
  352.0 278.4 %all-gather.5.cloned.1.call-done = bf16[8192,2048]{1,0:T(8,128)(2,1)} async-done(((bf16[1024,2048]{1,0:T(8,128)(2,1)}), bf16[8192,2048]{1,0:T(8,128)(2,1)}) %all-gather.5.cloned.1.call-update) | async-done | bytes 33554448 | tf_op jit(solution)/shard_map/all_gather | solution.py:50
  630.4 24.8 %fusion.8 = f32[512,2048]{1,0:T(8,128)} fusion(bf16[512,8192]{1,0:T(8,128)(2,1)} %constant_dynamic-update-slice_fusion, bf16[8192,2048]{1,0:T(8,128)(2,1)} %all-gather.5.cloned.1.call-done), kind=kOutput, calls=%fused_computation.15 | convolution fusion | flops 17181966336 | bytes 46137344 | tf_op jit(solution)/shard_map/dot_general | solution.py:48
  655.2 5.3 copy.32
  660.5 0.0 collective-permute-done.5
  660.5 2.2 add_select_fusion
  662.7 0.8 collective-permute-start.7
  663.5 10.7 %fusion = f32[32,64,512]{2,1,0:T(8,128)S(1)} fusion(bf16[512,32,64]{0,2,1:T(8,128)(2,1)S(1)} %bitcast.73, f32[512,512]{1,0:T(8,128)S(1)} %copy-done.10, f32[32,512]{1,0:T(8,128)S(1)} %copy-done.12, pred[512,512]{1,0:T(8,128)(4,1)S(1)} %copy-done.11), kind=kOutput, calls=%fused_computation.3 | convolution fusion | flops 1124073472 | bytes 7667712 | tf_op jit(solution)/shard_map/hts,shp->thp/dot_general | solution.py:68
  674.2 1.6 bitcast_dynamic-update-slice_fusion.3
  675.8 1.5 bitcast_dynamic-update-slice_fusion.2
  677.3 76.2 %collective-permute-done.7 = f32[32,64,256]{2,1,0:T(8,128)S(1)} collective-permute-done((f32[32,64,256]{2,1,0:T(8,128)S(1)}, f32[32,64,256]{2,1,0:T(8,128)S(1)}, u32[]{:S(2)}, u32[]{:S(2)}) %collective-permute-start.7) | collective-permute-done | bytes 2097184 | tf_op jit(solution)/shard_map/ppermute | solution.py:25
  753.5 1.6 bitcast_dynamic-update-slice_fusion.1
  755.1 1.6 broadcast_dynamic-update-slice_fusion
  756.7 1.6 bitcast_dynamic-update-slice_fusion
  758.3 14.6 %multiply_reduce_fusion = f32[512,32,64]{0,2,1:T(8,128)S(1)} fusion(f32[512,32,5]{0,1,2:T(8,128)S(1)} %multiply_bitcast_fusion, f32[5,32,64,256]{3,2,1,0:T(8,128)} %bitcast_dynamic-update-slice_fusion, bf16[512,1,1,256]{3,2,1,0:T(2,128)(2,1)S(1)} %constant_dynamic-slice_fusion.1), kind=kOutput, calls=%fused_computation.1 | convolution fusion | flops 16115564544 | bytes 15269888 | tf_op jit(solution)/shard_map/tn,lhpn->tlhp/dot_general | solution.py:100
  773.0 2.4 multiply_reduce_fusion.1
  775.4 0.0 copy-start.1
  775.5 0.7 multiply_convert_fusion.4
  776.1 2.4 copy.33
  (34 shorter events, 0.2 us)
Async XLA Ops:
  6.5 49.6 %copy-start = (f32[512,32]{0,1:T(8,128)S(1)}, f32[512,32]{0,1:T(8,128)}, u32[]{:S(2)}) copy-start(f32[512,32]{0,1:T(8,128)} %param.13) | copy-start | bytes 196612
  6.5 97.3 %copy-start.7 = (bf16[512,2,4,256]{3,2,1,0:T(4,128)(2,1)S(1)}, bf16[512,2,4,256]{3,2,1,0:T(4,128)(2,1)}, u32[]{:S(2)}) copy-start(bf16[512,2,4,256]{3,2,1,0:T(4,128)(2,1)} %param.12) | copy-start | bytes 6291460
  6.5 290.7 %all-gather.3.cloned.1.call-start = ((), (), s32[]{:S(2)}) async-start(), calls=%async_computation | async-start | bytes 37748736 | tf_op jit(solution)/shard_map/all_gather | solution.py:45
  7.3 623.1 %all-gather.5.cloned.1.call-start = ((), (), s32[]{:S(2)}) async-start(), calls=%async_computation.1 | async-start | bytes 37748736 | tf_op jit(solution)/shard_map/all_gather | solution.py:50
  8.0 47.8 %collective-permute-start = (bf16[512,2048]{1,0:T(8,128)(2,1)}, bf16[512,2048]{1,0:T(8,128)(2,1)}, u32[]{:S(2)}, u32[]{:S(2)}) collective-permute-start(bf16[512,2048]{1,0:T(8,128)(2,1)} %param.9), channel_id=1, source_target_pairs={{0,1},{1,2},{2,3},{3,0},{4,5},{5,6},{6,7},{7,4},{8,9},{9,10},{10,1... | collective-permute-start | bytes 6291464 | tf_op jit(solution)/shard_map/ppermute | solution.py:19
  55.8 46.9 %collective-permute-start.1 = (bf16[512,2048]{1,0:T(8,128)(2,1)}, bf16[512,2048]{1,0:T(8,128)(2,1)}, u32[]{:S(2)}, u32[]{:S(2)}) collective-permute-start(bf16[512,2048]{1,0:T(8,128)(2,1)} %collective-permute-done), channel_id=1, source_target_pairs={{0,1},{1,2},{2,3},{3,0},{4,5},{5,6},{6,7},{7,4},{8,9},{9,10},{10,1... | collective-permute-start | bytes 6291464 | tf_op jit(solution)/shard_map/ppermute | solution.py:19
  102.7 46.0 %collective-permute-start.2 = (bf16[512,2048]{1,0:T(8,128)(2,1)}, bf16[512,2048]{1,0:T(8,128)(2,1)}, u32[]{:S(2)}, u32[]{:S(2)}) collective-permute-start(bf16[512,2048]{1,0:T(8,128)(2,1)} %collective-permute-done.1), channel_id=1, source_target_pairs={{0,1},{1,2},{2,3},{3,0},{4,5},{5,6},{6,7},{7,4},{8,9},{9,10},{10,1... | collective-permute-start | bytes 6291464 | tf_op jit(solution)/shard_map/ppermute | solution.py:19
  106.9 4.3 copy-start.8
  325.8 1.3 copy-start.5
  327.1 15.0 %copy-start.13 = (f32[2048]{0:T(1024)S(1)}, f32[2048]{0:T(1024)}, u32[]{:S(2)}) copy-start(f32[2048]{0:T(1024)} %param.17) | copy-start | bytes 24580
  331.1 13.1 %collective-permute-start.3 = (f32[32,64,256]{2,1,0:T(8,128)}, f32[32,64,256]{2,1,0:T(8,128)S(1)}, u32[]{:S(2)}, u32[]{:S(2)}) collective-permute-start(f32[32,64,256]{2,1,0:T(8,128)} %fusion.2), channel_id=1, source_target_pairs={{0,4},{4,0},{8,12},{12,8},{16,20},{20,16},{24,28},{28,24},{1,5},{5... | collective-permute-start | bytes 6291464 | tf_op jit(solution)/shard_map/ppermute | solution.py:25
  331.3 6.0 collective-permute-start.4
  337.3 3.0 collective-permute-start.6
  340.3 3.9 collective-permute-start.8
  344.2 1.3 copy-start.3
  349.0 311.5 %collective-permute-start.5 = (f32[32,64,256]{2,1,0:T(8,128)}, f32[32,64,256]{2,1,0:T(8,128)S(1)}, u32[]{:S(2)}, u32[]{:S(2)}) collective-permute-start(f32[32,64,256]{2,1,0:T(8,128)} %add_select_fusion.1), channel_id=1, source_target_pairs={{0,8},{4,12},{8,0},{12,4},{16,24},{20,28},{24,16},{28,20},{1,9},{5... | collective-permute-start | bytes 6291464 | tf_op jit(solution)/shard_map/ppermute | solution.py:25
  660.5 3.0 copy-start.6
  660.5 3.0 copy-start.10
  660.5 3.0 copy-start.11
  660.5 3.0 copy-start.12
  662.7 90.8 %collective-permute-start.7 = (f32[32,64,256]{2,1,0:T(8,128)S(1)}, f32[32,64,256]{2,1,0:T(8,128)S(1)}, u32[]{:S(2)}, u32[]{:S(2)}) collective-permute-start(f32[32,64,256]{2,1,0:T(8,128)S(1)} %add_select_fusion), channel_id=1, source_target_pairs={{0,16},{4,20},{8,24},{12,28},{16,0},{20,4},{24,8},{28,12},{1,17},{... | collective-permute-start | bytes 6291464 | tf_op jit(solution)/shard_map/ppermute | solution.py:25
  663.5 10.7 %copy-start.4 = (f32[32,64,256]{2,1,0:T(8,128)S(1)}, f32[32,64,256]{2,1,0:T(8,128)}, u32[]{:S(2)}) copy-start(f32[32,64,256]{2,1,0:T(8,128)} %copy-done.3) | copy-start | bytes 6291460
  677.3 79.4 %copy-start.9 = (f32[32,64,256]{2,1,0:T(8,128)S(1)}, f32[32,64,256]{2,1,0:T(8,128)}, u32[]{:S(2)}) copy-start(f32[32,64,256]{2,1,0:T(8,128)} %param.15) | copy-start | bytes 6291460
  758.3 14.7 %copy-start.2 = (f32[512,2048]{0,1:T(8,128)S(1)}, f32[512,2048]{0,1:T(8,128)}, u32[]{:S(2)}) copy-start(f32[512,2048]{0,1:T(8,128)} %copy.32) | copy-start | bytes 12582916
  758.3 14.7 %copy-start.14 = (f32[32]{0:T(128)S(1)}, f32[32]{0:T(128)}, u32[]{:S(2)}) copy-start(f32[32]{0:T(128)} %param.16) | copy-start | bytes 388
  775.4 3.1 copy-start.1
Sparse Core Ops, SparseCore 0:
  8.9 288.2 all-gather.2
  298.8 331.5 all-gather.4
